TPU v7x, 32 devices: a whole 2x2x4 slice. The times are simulated.
32 devices in a mesh: pix: 8 (over y, x, core), tm: 4 (over z).
Axes of the slice: x: 2, y: 2, z: 4, core: 2. Of those that a mesh axis runs over, the one named last changes fastest.
Arguments:
- raw_movie: float32 [64, 256, 2048], P('pix', None, 'tm'), may hold values from 0.05 to 2
- footprints: float32 [256, 16384], P('tm', 'pix'), may hold values from 0.05 to 1
- traces: float32 [256, 2048], P('pix', 'tm'), may hold values from 0.05 to 1
Outputs:
- denoised: float32 [64, 256, 2048], P('pix', None, 'tm')
- new_footprints: float32 [256, 16384], P('tm', 'pix')
- new_traces: float32 [256, 2048], P('pix', 'tm')
All inputs are finite; a program needn't handle non-finite values.
Results may differ from a plain program's by a relative error of at most 0.00013.
Values sent between devices are 32-bit elements; how exact they have to be, the bound alone decides.
No kernel may reach another device: no remote copies, remote signals or barrier semaphores. Data moves between devices by JAX's collectives and lax.ppermute only.
A program may use at most 64 MiB of HBM per device.

v0:
```python
import jax
import jax.numpy as jnp
from jax import lax
from jax.sharding import PartitionSpec as P

edge_scale = 0.5
step_size = 0.24


def with_halo(cells, sides, width):
    for axis, dim in sides:
        count = lax.axis_size(axis)
        ends = count - 1
        head = lax.slice_in_dim(cells, 0, width, axis=dim)
        tail = lax.slice_in_dim(cells, cells.shape[dim] - width, cells.shape[dim], axis=dim)
        cells = jnp.concatenate(
            [
                lax.ppermute(tail, axis, [(i, (i + 1) % count) for i in range(ends)]),
                cells,
                lax.ppermute(head, axis, [((i + 1) % count, i) for i in range(ends)]),
            ],
            axis=dim,
        )
    return cells


def flux_term(change):
    return change / (1.0 + change / edge_scale * (change / edge_scale))


def substep(extended):
    middle = extended[1:-1]
    padded = jnp.pad(middle, ((0, 0), (1, 1), (0, 0)))
    summed = flux_term(extended[:-2] - middle) + flux_term(extended[2:] - middle)
    summed = summed + flux_term(padded[:, :-2] - middle) + flux_term(padded[:, 2:] - middle)
    return middle + step_size * summed


def matmul_hi(left, right):
    return jnp.dot(left, right, precision=lax.Precision.HIGHEST, preferred_element_type=jnp.float32)


def contract_last(left, right):
    return lax.dot_general(
        left,
        right,
        (((1,), (1,)), ((), ())),
        precision=lax.Precision.HIGHEST,
        preferred_element_type=jnp.float32,
    )


def body(raw_movie, footprints, traces):
    row_count = raw_movie.shape[0]
    col_count = raw_movie.shape[1]
    frame_count = raw_movie.shape[2]
    current = raw_movie
    for repeat in range(4):
        extended = with_halo(current, (("pix", 0),), 1)
        current = substep(extended)
    pixels = current.reshape(row_count * col_count, frame_count)
    foot_full = lax.all_gather(footprints, "tm", axis=0, tiled=True)
    trace_full = lax.all_gather(traces, "pix", axis=0, tiled=True)
    part = foot_full
    merged = lax.psum_scatter(
        jnp.concatenate([matmul_hi(part, pixels), contract_last(part, foot_full)], axis=1),
        "pix",
        scatter_dimension=0,
        tiled=True,
    )
    numerator = merged[:, :frame_count]
    gram_rows = merged[:, frame_count:]
    new_traces = traces * numerator / matmul_hi(gram_rows, trace_full)
    new_full = lax.all_gather(new_traces, "pix", axis=0, tiled=True)
    part = new_full
    joined = lax.psum_scatter(
        jnp.concatenate([contract_last(part, pixels), contract_last(part, new_full)], axis=1),
        "tm",
        scatter_dimension=0,
        tiled=True,
    )
    foot_numerator = joined[:, : row_count * col_count]
    trace_rows = joined[:, row_count * col_count :]
    new_footprints = footprints * foot_numerator / matmul_hi(trace_rows, foot_full)
    return (current, new_footprints, new_traces)


def solution(mesh):
    placed = (P("pix", None, "tm"), P("tm", "pix"), P("pix", "tm"))
    return jax.shard_map(
        body,
        mesh=mesh,
        in_specs=placed,
        out_specs=(P("pix", None, "tm"), P("tm", "pix"), P("pix", "tm")),
        check_vma=False,
    )
```

profile of v0, /device:TPU:0, one launch (start us, length us, event | category | flops | bytes accessed | tf_op | source)
XLA Modules:
  0.0 233.4 jit_solution(9281021780774878681)
XLA Ops:
  7.2 0.0 all-gather.2.cloned.1.call-start
  7.2 1.3 fusion.13
  8.5 2.4 %collective-permute-start = (f32[1,256,512]{2,1,0:T(8,128)S(1)}, f32[1,256,512]{2,1,0:T(8,128)S(1)}, u32[]{:S(2)}, u32[]{:S(2)}) collective-permute-start(f32[1,256,512]{2,1,0:T(8,128)S(1)} %get-tuple-element.12), channel_id=1, source_target_pairs={{0,4},{4,8},{8,12},{12,16},{16,20},{20,24},{24,28},{1,5},{5,9},{9,... | collective-permute-start | bytes 1572872 | tf_op jit(solution)/shard_map/ppermute | solution.py:18
  10.9 1.3 collective-permute-start.1
  12.2 0.2 collective-permute-done
  12.4 4.4 %collective-permute-done.1 = f32[1,256,512]{2,1,0:T(8,128)S(1)} collective-permute-done((f32[1,256,512]{2,1,0:T(8,128)S(1)}, f32[1,256,512]{2,1,0:T(8,128)S(1)}, u32[]{:S(2)}, u32[]{:S(2)}) %collective-permute-start.1) | collective-permute-done | bytes 524320 | tf_op jit(solution)/shard_map/ppermute | solution.py:20
  16.8 9.8 %multiply_add_fusion.3 = f32[8,256,512]{2,1,0:T(8,128)S(1)} fusion(f32[8,256,512]{2,1,0:T(8,128)} %param.3, f32[1,256,512]{2,1,0:T(8,128)S(1)} %collective-permute-done.1, f32[1,256,512]{2,1,0:T(8,128)S(1)} %collective-permute-done), kind=kLoop, calls=%fused_computation.19 | loop fusion | flops 28311552 | bytes 9437184 | tf_op jit(solution)/shard_map/add | solution.py:36
  26.6 0.1 fusion.12
  26.7 12.0 %collective-permute-start.2 = (f32[1,256,512]{2,1,0:T(8,128)S(1)}, f32[1,256,512]{2,1,0:T(8,128)S(1)}, u32[]{:S(2)}, u32[]{:S(2)}) collective-permute-start(f32[1,256,512]{2,1,0:T(8,128)S(1)} %get-tuple-element.10), channel_id=1, source_target_pairs={{0,4},{4,8},{8,12},{12,16},{16,20},{20,24},{24,28},{1,5},{5,9},{9,... | collective-permute-start | bytes 1572872 | tf_op jit(solution)/shard_map/ppermute | solution.py:18
  38.7 1.3 collective-permute-start.3
  40.0 0.2 collective-permute-done.2
  40.2 2.3 collective-permute-done.3
  42.5 4.5 %multiply_add_fusion.2 = f32[8,256,512]{2,1,0:T(8,128)S(1)} fusion(f32[8,256,512]{2,1,0:T(8,128)S(1)} %multiply_add_fusion.3, f32[1,256,512]{2,1,0:T(8,128)S(1)} %collective-permute-done.3, f32[1,256,512]{2,1,0:T(8,128)S(1)} %collective-permute-done.2), kind=kLoop, calls=%fused_computation.18 | loop fusion | flops 28311552 | bytes 9437184 | tf_op jit(solution)/shard_map/add | solution.py:36
  47.0 0.0 copy-start.2
  47.1 2.0 copy-done.2
  49.1 0.1 fusion.11
  49.1 11.5 %collective-permute-start.4 = (f32[1,256,512]{2,1,0:T(8,128)S(1)}, f32[1,256,512]{2,1,0:T(8,128)S(1)}, u32[]{:S(2)}, u32[]{:S(2)}) collective-permute-start(f32[1,256,512]{2,1,0:T(8,128)S(1)} %get-tuple-element.8), channel_id=1, source_target_pairs={{0,4},{4,8},{8,12},{12,16},{16,20},{20,24},{24,28},{1,5},{5,9},{9,... | collective-permute-start | bytes 1572872 | tf_op jit(solution)/shard_map/ppermute | solution.py:18
  60.6 1.3 collective-permute-start.5
  61.9 0.0 all-gather.2.cloned.1.call-update
  62.0 0.0 reduce-scatter.7.cloned.1.call-start
  62.0 0.1 collective-permute-done.4
  62.1 2.3 collective-permute-done.5
  64.4 10.0 %multiply_add_fusion.1 = f32[8,256,512]{2,1,0:T(8,128)S(1)} fusion(f32[8,256,512]{2,1,0:T(8,128)} %copy-done.2, f32[1,256,512]{2,1,0:T(8,128)S(1)} %collective-permute-done.5, f32[1,256,512]{2,1,0:T(8,128)S(1)} %collective-permute-done.4), kind=kLoop, calls=%fused_computation.17 | loop fusion | flops 28311552 | bytes 9437184 | tf_op jit(solution)/shard_map/add | solution.py:36
  74.4 0.1 fusion.10
  74.5 10.5 %collective-permute-start.6 = (f32[1,256,512]{2,1,0:T(8,128)S(1)}, f32[1,256,512]{2,1,0:T(8,128)S(1)}, u32[]{:S(2)}, u32[]{:S(2)}) collective-permute-start(f32[1,256,512]{2,1,0:T(8,128)S(1)} %get-tuple-element.6), channel_id=1, source_target_pairs={{0,4},{4,8},{8,12},{12,16},{16,20},{20,24},{24,28},{1,5},{5,9},{9,... | collective-permute-start | bytes 1572872 | tf_op jit(solution)/shard_map/ppermute | solution.py:18
  85.0 1.5 collective-permute-start.7
  86.5 0.0 collective-permute-done.6
  86.5 2.3 collective-permute-done.7
  88.8 5.5 %multiply_add_fusion = f32[8,256,512]{2,1,0:T(8,128)} fusion(f32[8,256,512]{2,1,0:T(8,128)S(1)} %multiply_add_fusion.1, f32[1,256,512]{2,1,0:T(8,128)S(1)} %collective-permute-done.7, f32[1,256,512]{2,1,0:T(8,128)S(1)} %collective-permute-done.6), kind=kLoop, calls=%fused_computation.16 | loop fusion | flops 28311552 | bytes 9437184 | tf_op jit(solution)/shard_map/add | solution.py:36
  94.3 14.5 %all-gather.2.cloned.1.call-done = f32[256,2048]{1,0:T(8,128)} async-done(((f32[64,2048]{1,0:T(8,128)}), f32[256,2048]{1,0:T(8,128)}) %all-gather.2.cloned.1.call-update) | async-done | bytes 2097168 | tf_op jit(solution)/shard_map/all_gather | solution.py:62
  108.8 4.2 %fusion.14 = f32[256,256]{0,1:T(8,128)S(1)} fusion(f32[256,2048]{1,0:T(8,128)} %all-gather.2.cloned.1.call-done), kind=kOutput, calls=%fused_computation.33 | convolution fusion | flops 1610612736 | bytes 2359296 | tf_op jit(solution)/shard_map/dot_general | solution.py:44
  113.0 0.0 copy-start.4
  113.1 8.4 %convolution_bitcast_fusion = f32[256,512]{0,1:T(8,128)S(1)} fusion(f32[2048,512]{1,0:T(8,128)S(1)} %bitcast.15, f32[256,2048]{1,0:T(8,128)} %all-gather.2.cloned.1.call-done), kind=kOutput, calls=%fused_computation.22 | convolution fusion | flops 3221225472 | bytes 6815744 | tf_op jit(solution)/shard_map/dot_general | solution.py:40
  121.5 0.1 pad_maximum_fusion.9
  121.6 1.1 copy.13
  122.7 0.0 reduce-scatter.7.cloned.1.call-update
  122.7 0.0 reduce-scatter.5.cloned.1.call-start
  122.8 9.8 %all_gather.10 = f32[256,512]{1,0:T(8,128)S(1)} all-gather(f32[32,512]{1,0:T(8,128)S(1)} %copy-done.4), channel_id=1, replica_groups=mesh['pix'=8,'tm'=4] {'pix'}, dimensions={0}, use_global_device_ids=true | all-gather | bytes 589824 | tf_op jit(solution)/shard_map/all_gather | solution.py:63
  132.6 24.0 %reduce-scatter.7.cloned.1.call-done = f32[32,768]{1,0:T(8,128)} async-done(((f32[256,768]{1,0:T(8,128)}), f32[32,768]{1,0:T(8,128)}) %reduce-scatter.7.cloned.1.call-update) | async-done | bytes 98320 | tf_op jit(solution)/shard_map/reduce_scatter | solution.py:65
  156.7 1.3 convolution_divide_fusion.1
  157.9 0.0 copy-start.5
  157.9 10.0 %all_gather.11 = f32[256,512]{1,0:T(8,128)S(1)} all-gather(f32[32,512]{1,0:T(8,128)S(1)} %convolution_divide_fusion.1), channel_id=1, replica_groups=mesh['pix'=8,'tm'=4] {'pix'}, dimensions={0}, use_global_device_ids=true | all-gather | bytes 589824 | tf_op jit(solution)/shard_map/all_gather | solution.py:74
  168.0 5.5 %fusion.15 = f32[256,2048]{1,0:T(8,128)S(1)} fusion(f32[256,512]{1,0:T(8,128)S(1)} %all_gather.11, f32[2048,512]{1,0:T(8,128)} %bitcast.14), kind=kOutput, calls=%fused_computation.34 | convolution fusion | flops 3221225472 | bytes 6815744 | tf_op jit(solution)/shard_map/dot_general | solution.py:44
  173.5 0.6 fusion.16
  174.1 1.6 pad_maximum_fusion.8
  175.7 0.0 reduce-scatter.5.cloned.1.call-update
  175.8 47.9 %reduce-scatter.5.cloned.1.call-done = f32[64,2304]{1,0:T(8,128)} async-done(((f32[256,2304]{1,0:T(8,128)}), f32[64,2304]{1,0:T(8,128)}) %reduce-scatter.5.cloned.1.call-update) | async-done | bytes 589840 | tf_op jit(solution)/shard_map/reduce_scatter | solution.py:76
  223.6 3.3 %convolution_divide_fusion = f32[64,2048]{1,0:T(8,128)} fusion(f32[256,2048]{1,0:T(8,128)S(1)} %copy-done.1, f32[64,2048]{1,0:T(8,128)S(1)} %copy-done.3, f32[64,2304]{1,0:T(8,128)} %reduce-scatter.5.cloned.1.call-done), kind=kOutput, calls=%fused_computation.21 | convolution fusion | flops 402915328 | bytes 3735552 | tf_op jit(solution)/shard_map/dot_general | solution.py:40
  (8 shorter events, 0.0 us)
Async XLA Ops:
  7.2 101.6 %all-gather.2.cloned.1.call-start = ((), (), s32[]{:S(2)}) async-start(), calls=%async_computation.2 | async-start | bytes 2621440 | tf_op jit(solution)/shard_map/all_gather | solution.py:62
  8.5 3.9 %collective-permute-start = (f32[1,256,512]{2,1,0:T(8,128)S(1)}, f32[1,256,512]{2,1,0:T(8,128)S(1)}, u32[]{:S(2)}, u32[]{:S(2)}) collective-permute-start(f32[1,256,512]{2,1,0:T(8,128)S(1)} %get-tuple-element.12), channel_id=1, source_target_pairs={{0,4},{4,8},{8,12},{12,16},{16,20},{20,24},{24,28},{1,5},{5,9},{9,... | collective-permute-start | bytes 1572872 | tf_op jit(solution)/shard_map/ppermute | solution.py:18
  10.9 5.9 %collective-permute-start.1 = (f32[1,256,512]{2,1,0:T(8,128)S(1)}, f32[1,256,512]{2,1,0:T(8,128)S(1)}, u32[]{:S(2)}, u32[]{:S(2)}) collective-permute-start(f32[1,256,512]{2,1,0:T(8,128)S(1)} %get-tuple-element.13), channel_id=1, source_target_pairs={{4,0},{8,4},{12,8},{16,12},{20,16},{24,20},{28,24},{5,1},{9,5},{13... | collective-permute-start | bytes 1572872 | tf_op jit(solution)/shard_map/ppermute | solution.py:20
  26.7 13.5 %collective-permute-start.2 = (f32[1,256,512]{2,1,0:T(8,128)S(1)}, f32[1,256,512]{2,1,0:T(8,128)S(1)}, u32[]{:S(2)}, u32[]{:S(2)}) collective-permute-start(f32[1,256,512]{2,1,0:T(8,128)S(1)} %get-tuple-element.10), channel_id=1, source_target_pairs={{0,4},{4,8},{8,12},{12,16},{16,20},{20,24},{24,28},{1,5},{5,9},{9,... | collective-permute-start | bytes 1572872 | tf_op jit(solution)/shard_map/ppermute | solution.py:18
  38.7 3.8 %collective-permute-start.3 = (f32[1,256,512]{2,1,0:T(8,128)S(1)}, f32[1,256,512]{2,1,0:T(8,128)S(1)}, u32[]{:S(2)}, u32[]{:S(2)}) collective-permute-start(f32[1,256,512]{2,1,0:T(8,128)S(1)} %get-tuple-element.11), channel_id=1, source_target_pairs={{4,0},{8,4},{12,8},{16,12},{20,16},{24,20},{28,24},{5,1},{9,5},{13... | collective-permute-start | bytes 1572872 | tf_op jit(solution)/shard_map/ppermute | solution.py:20
  47.0 2.0 copy-start.2
  49.1 13.0 %collective-permute-start.4 = (f32[1,256,512]{2,1,0:T(8,128)S(1)}, f32[1,256,512]{2,1,0:T(8,128)S(1)}, u32[]{:S(2)}, u32[]{:S(2)}) collective-permute-start(f32[1,256,512]{2,1,0:T(8,128)S(1)} %get-tuple-element.8), channel_id=1, source_target_pairs={{0,4},{4,8},{8,12},{12,16},{16,20},{20,24},{24,28},{1,5},{5,9},{9,... | collective-permute-start | bytes 1572872 | tf_op jit(solution)/shard_map/ppermute | solution.py:18
  60.6 3.8 %collective-permute-start.5 = (f32[1,256,512]{2,1,0:T(8,128)S(1)}, f32[1,256,512]{2,1,0:T(8,128)S(1)}, u32[]{:S(2)}, u32[]{:S(2)}) collective-permute-start(f32[1,256,512]{2,1,0:T(8,128)S(1)} %get-tuple-element.9), channel_id=1, source_target_pairs={{4,0},{8,4},{12,8},{16,12},{20,16},{24,20},{28,24},{5,1},{9,5},{13... | collective-permute-start | bytes 1572872 | tf_op jit(solution)/shard_map/ppermute | solution.py:20
  62.0 94.7 %reduce-scatter.7.cloned.1.call-start = ((), (), s32[]{:S(2)}) async-start(), calls=%async_computation.4 | async-start | bytes 884736 | tf_op jit(solution)/shard_map/reduce_scatter | solution.py:65
  74.5 12.0 %collective-permute-start.6 = (f32[1,256,512]{2,1,0:T(8,128)S(1)}, f32[1,256,512]{2,1,0:T(8,128)S(1)}, u32[]{:S(2)}, u32[]{:S(2)}) collective-permute-start(f32[1,256,512]{2,1,0:T(8,128)S(1)} %get-tuple-element.6), channel_id=1, source_target_pairs={{0,4},{4,8},{8,12},{12,16},{16,20},{20,24},{24,28},{1,5},{5,9},{9,... | collective-permute-start | bytes 1572872 | tf_op jit(solution)/shard_map/ppermute | solution.py:18
  85.0 3.8 %collective-permute-start.7 = (f32[1,256,512]{2,1,0:T(8,128)S(1)}, f32[1,256,512]{2,1,0:T(8,128)S(1)}, u32[]{:S(2)}, u32[]{:S(2)}) collective-permute-start(f32[1,256,512]{2,1,0:T(8,128)S(1)} %get-tuple-element.7), channel_id=1, source_target_pairs={{4,0},{8,4},{12,8},{16,12},{20,16},{24,20},{28,24},{5,1},{9,5},{13... | collective-permute-start | bytes 1572872 | tf_op jit(solution)/shard_map/ppermute | solution.py:20
  108.8 4.2 %copy-start = (f32[8,256,512]{2,1,0:T(8,128)S(1)}, f32[8,256,512]{2,1,0:T(8,128)}, u32[]{:S(2)}) copy-start(f32[8,256,512]{2,1,0:T(8,128)} %multiply_add_fusion) | copy-start | bytes 12582916
  113.0 9.7 %copy-start.4 = (f32[32,512]{1,0:T(8,128)S(1)}, f32[32,512]{1,0:T(8,128)}, u32[]{:S(2)}) copy-start(f32[32,512]{1,0:T(8,128)} %param.5) | copy-start | bytes 196612
  122.7 100.9 %reduce-scatter.5.cloned.1.call-start = ((), (), s32[]{:S(2)}) async-start(), calls=%async_computation.3 | async-start | bytes 2949120 | tf_op jit(solution)/shard_map/reduce_scatter | solution.py:76
  157.9 16.2 %copy-start.5 = (f32[32,512]{1,0:T(8,128)}, f32[32,512]{1,0:T(8,128)S(1)}, u32[]{:S(2)}) copy-start(f32[32,512]{1,0:T(8,128)S(1)} %convolution_divide_fusion.1) | copy-start | bytes 196612
  173.5 50.1 %copy-start.1 = (f32[256,2048]{1,0:T(8,128)S(1)}, f32[256,2048]{1,0:T(8,128)}, u32[]{:S(2)}) copy-start(f32[256,2048]{1,0:T(8,128)} %all-gather.2.cloned.1.call-done) | copy-start | bytes 6291460
  173.5 50.1 %copy-start.3 = (f32[64,2048]{1,0:T(8,128)S(1)}, f32[64,2048]{1,0:T(8,128)}, u32[]{:S(2)}) copy-start(f32[64,2048]{1,0:T(8,128)} %param.4) | copy-start | bytes 1572868
Sparse Core Ops, SparseCore 0:
  62.1 46.6 all-gather.1
  122.9 33.7 reduce-scatter.6
  175.9 47.6 reduce-scatter.4
where the time goes:
time: 234 us; the launch traced here: 233 us
  waiting for transfers between devices  98.3 us (42%)
  starting transfers between devices  41.9 us (18%)
  other arithmetic  31.5 us (13%)
  matrix products  23.3 us (10%)
  blocking collectives  19.8 us (8%)
  between operations  14 us (6%)
  local copies, waits for them, and re-layouts  4.67 us (2%)
    reduce_scatter x1, waiting for transfers between devices, body(): lax.psum_scatter(jnp.concatenate([contract_last(part, pixels), contract_l...  47.9 us
    ppermute x4, starting transfers between devices, with_halo(): lax.ppermute(tail, axis, [(i, (i + 1) % count) for i in range(ends)])  36.4 us
    add x4, other arithmetic, substep(): return middle + step_size * summed  29.8 us
    reduce_scatter x1, waiting for transfers between devices, body(): lax.psum_scatter(jnp.concatenate([matmul_hi(part, pixels), contract_last(...  24 us
    all_gather x1, waiting for transfers between devices, body(): foot_full = lax.all_gather(footprints, 'tm', axis=0, tiled=True)  14.5 us
    dot_general x3, matrix products, matmul_hi(): jnp.dot(left, right, precision=lax.Precision.HIGHEST, preferred_element_t...  13 us
    ppermute x4, waiting for transfers between devices, with_halo(): lax.ppermute(head, axis, [((i + 1) % count, i) for i in range(ends)])  11.3 us
    dot_general x3, matrix products, contract_last(): lax.dot_general(left, right, (((1,), (1,)), ((), ())), precision=lax.Prec...  10.3 us
  transfers between devices with their start and end apart: 11, of which 10 were waited for; matrix products, arithmetic and copies ran while one was open for 7% of the time, Pallas kernels for 0%

commit v1 on v0

--- a/solution.py
+++ b/solution.py
@@ -59,7 +59,12 @@
         extended = with_halo(current, (("pix", 0),), 1)
         current = substep(extended)
     pixels = current.reshape(row_count * col_count, frame_count)
-    foot_full = lax.all_gather(footprints, "tm", axis=0, tiled=True)
+    ring = [footprints]
+    for hop in range(3):
+        ring.append(lax.ppermute(ring[-1], "tm", [(dev, (dev + 1) % 4) for dev in range(4)]))
+    foot_full = jnp.roll(
+        jnp.concatenate(ring[::-1], axis=0), (lax.axis_index("tm") + 1) * ring[0].shape[0], axis=0
+    )
     trace_full = lax.all_gather(traces, "pix", axis=0, tiled=True)
     part = foot_full
     merged = lax.psum_scatter(

time: 234 us -> 221 us (0.944)
  waiting for transfers between devices: 98.3 us -> 73.4 us
  blocking collectives: 19.8 us -> 36.6 us
  matrix products: 23.3 us -> 16.8 us
    all_gather x1, blocking collectives: 9.81 us -> 26.5 us  [body(): trace_full = lax.all_gather(traces, 'pix', axis=0, tiled=True)]
    all_gather x1 -> x0, waiting for transfers between devices: 14.5 us -> none  [body(): foot_full = lax.all_gather(footprints, 'tm', axis=0, tiled=True)]
    ppermute x4, waiting for transfers between devices: 11.3 us -> 0.01 us  [with_halo(): lax.ppermute(head, axis, [((i + 1) % count, i) for i in range(ends)])]
    ppermute x0 -> x3, starting transfers between devices: none -> 6.36 us  [body(): lax.ppermute(ring[-1], 'tm', [(dev, (dev + 1) % 4) for dev in range(4)])]
    ppermute x4, starting transfers between devices: 36.4 us -> 30.6 us  [with_halo(): lax.ppermute(tail, axis, [(i, (i + 1) % count) for i in range(ends)])]
    dot_general x3, matrix products: 13 us -> 8.83 us  [matmul_hi(): jnp.dot(left, right, precision=lax.Precision.HIGHEST, preferred_element_t...]
  transfers between devices with their start and end apart: 11 -> 13, of which waited for: 10 -> 2; matrix products, arithmetic and copies ran while one was open for 7% -> 12% of each run, Pallas kernels for 0% -> 0%
where the time goes in v1:
time: 221 us
  waiting for transfers between devices  73.4 us (33%)
  starting transfers between devices  42.3 us (19%)
  blocking collectives  36.6 us (17%)
  other arithmetic  31.5 us (14%)
  matrix products  16.8 us (8%)
  between operations  14.4 us (7%)
  local copies, waits for them, and re-layouts  5.8 us (3%)
    reduce_scatter x1, waiting for transfers between devices, body(): lax.psum_scatter(jnp.concatenate([contract_last(part, pixels), contract_l...  47.8 us
    ppermute x4, starting transfers between devices, with_halo(): lax.ppermute(tail, axis, [(i, (i + 1) % count) for i in range(ends)])  30.6 us
    add x4, other arithmetic, substep(): return middle + step_size * summed  28.9 us
    all_gather x1, blocking collectives, body(): trace_full = lax.all_gather(traces, 'pix', axis=0, tiled=True)  26.5 us
    reduce_scatter x1, waiting for transfers between devices, body(): lax.psum_scatter(jnp.concatenate([matmul_hi(part, pixels), contract_last(...  25.6 us
    all_gather x1, blocking collectives, body(): new_full = lax.all_gather(new_traces, 'pix', axis=0, tiled=True)  10 us
    dot_general x3, matrix products, matmul_hi(): jnp.dot(left, right, precision=lax.Precision.HIGHEST, preferred_element_t...  8.83 us
    dot_general x3, matrix products, contract_last(): lax.dot_general(left, right, (((1,), (1,)), ((), ())), precision=lax.Prec...  8 us
  transfers between devices with their start and end apart: 13, of which 2 were waited for; matrix products, arithmetic and copies ran while one was open for 12% of the time, Pallas kernels for 0%

profile of v1, /device:TPU:0, one launch (start us, length us, event | category | flops | bytes accessed | tf_op | source)
XLA Modules:
  0.0 220.8 jit_solution(3521267773429894203)
XLA Ops:
  7.2 0.0 reduce-scatter.3.cloned.1.call-start
  7.2 1.3 fusion.21
  8.5 1.3 collective-permute-start.1
  9.8 3.1 %collective-permute-start = (f32[1,256,512]{2,1,0:T(8,128)S(1)}, f32[1,256,512]{2,1,0:T(8,128)S(1)}, u32[]{:S(2)}, u32[]{:S(2)}) collective-permute-start(f32[1,256,512]{2,1,0:T(8,128)S(1)} %get-tuple-element.9), channel_id=1, source_target_pairs={{0,4},{4,8},{8,12},{12,16},{16,20},{20,24},{24,28},{1,5},{5,9},{9,... | collective-permute-start | bytes 1572872 | tf_op jit(solution)/shard_map/ppermute | solution.py:18
  12.9 3.1 %collective-permute-start.8 = (f32[64,2048]{1,0:T(8,128)}, f32[64,2048]{1,0:T(8,128)S(1)}, u32[]{:S(2)}, u32[]{:S(2)}) collective-permute-start(f32[64,2048]{1,0:T(8,128)} %param.4), channel_id=1, source_target_pairs={{0,1},{1,2},{2,3},{3,0},{4,5},{5,6},{6,7},{7,4},{8,9},{9,10},{10,1... | collective-permute-start | bytes 1572872 | tf_op jit(solution)/shard_map/ppermute | solution.py:64
  16.0 0.0 collective-permute-done.1
  16.0 0.0 collective-permute-done
  16.0 9.8 %multiply_add_fusion.3 = f32[8,256,512]{2,1,0:T(8,128)S(1)} fusion(f32[8,256,512]{2,1,0:T(8,128)} %param.3, f32[1,256,512]{2,1,0:T(8,128)S(1)} %collective-permute-done.1, f32[1,256,512]{2,1,0:T(8,128)S(1)} %collective-permute-done), kind=kLoop, calls=%fused_computation.19 | loop fusion | flops 28311552 | bytes 9437184 | tf_op jit(solution)/shard_map/add | solution.py:36
  25.8 0.1 fusion.20
  25.9 1.3 collective-permute-start.3
  27.2 9.1 %collective-permute-start.2 = (f32[1,256,512]{2,1,0:T(8,128)S(1)}, f32[1,256,512]{2,1,0:T(8,128)S(1)}, u32[]{:S(2)}, u32[]{:S(2)}) collective-permute-start(f32[1,256,512]{2,1,0:T(8,128)S(1)} %get-tuple-element.7), channel_id=1, source_target_pairs={{0,4},{4,8},{8,12},{12,16},{16,20},{20,24},{24,28},{1,5},{5,9},{9,... | collective-permute-start | bytes 1572872 | tf_op jit(solution)/shard_map/ppermute | solution.py:18
  36.3 0.0 collective-permute-done.8
  36.3 1.6 collective-permute-start.9
  38.0 0.0 collective-permute-done.3
  38.0 0.0 collective-permute-done.2
  38.0 4.5 %multiply_add_fusion.2 = f32[8,256,512]{2,1,0:T(8,128)S(1)} fusion(f32[8,256,512]{2,1,0:T(8,128)S(1)} %multiply_add_fusion.3, f32[1,256,512]{2,1,0:T(8,128)S(1)} %collective-permute-done.3, f32[1,256,512]{2,1,0:T(8,128)S(1)} %collective-permute-done.2), kind=kLoop, calls=%fused_computation.18 | loop fusion | flops 28311552 | bytes 9437184 | tf_op jit(solution)/shard_map/add | solution.py:36
  42.5 0.0 copy-start.1
  42.5 2.0 copy-done.1
  44.5 0.1 fusion.19
  44.6 1.3 collective-permute-start.5
  45.9 8.7 %collective-permute-start.4 = (f32[1,256,512]{2,1,0:T(8,128)S(1)}, f32[1,256,512]{2,1,0:T(8,128)S(1)}, u32[]{:S(2)}, u32[]{:S(2)}) collective-permute-start(f32[1,256,512]{2,1,0:T(8,128)S(1)} %get-tuple-element.5), channel_id=1, source_target_pairs={{0,4},{4,8},{8,12},{12,16},{16,20},{20,24},{24,28},{1,5},{5,9},{9,... | collective-permute-start | bytes 1572872 | tf_op jit(solution)/shard_map/ppermute | solution.py:18
  54.7 0.0 collective-permute-done.9
  54.7 1.6 collective-permute-start.10
  56.3 0.0 collective-permute-done.5
  56.3 10.0 %multiply_add_fusion.1 = f32[8,256,512]{2,1,0:T(8,128)S(1)} fusion(f32[8,256,512]{2,1,0:T(8,128)} %copy-done.1, f32[1,256,512]{2,1,0:T(8,128)S(1)} %collective-permute-done.5, f32[1,256,512]{2,1,0:T(8,128)S(1)} %collective-permute-done.4), kind=kLoop, calls=%fused_computation.17 | loop fusion | flops 28311552 | bytes 9437184 | tf_op jit(solution)/shard_map/add | solution.py:36
  66.3 0.0 copy-start.3
  66.3 0.1 fusion.18
  66.4 1.4 collective-permute-start.7
  67.8 9.6 %collective-permute-start.6 = (f32[1,256,512]{2,1,0:T(8,128)S(1)}, f32[1,256,512]{2,1,0:T(8,128)S(1)}, u32[]{:S(2)}, u32[]{:S(2)}) collective-permute-start(f32[1,256,512]{2,1,0:T(8,128)S(1)} %get-tuple-element.3), channel_id=1, source_target_pairs={{0,4},{4,8},{8,12},{12,16},{16,20},{20,24},{24,28},{1,5},{5,9},{9,... | collective-permute-start | bytes 1572872 | tf_op jit(solution)/shard_map/ppermute | solution.py:18
  77.9 1.9 fusion.9
  79.8 4.6 %multiply_add_fusion = f32[8,256,512]{2,1,0:T(8,128)S(1)} fusion(f32[8,256,512]{2,1,0:T(8,128)S(1)} %multiply_add_fusion.1, f32[1,256,512]{2,1,0:T(8,128)S(1)} %collective-permute-done.7, f32[1,256,512]{2,1,0:T(8,128)S(1)} %collective-permute-done.6), kind=kLoop, calls=%fused_computation.16 | loop fusion | flops 28311552 | bytes 9437184 | tf_op jit(solution)/shard_map/add | solution.py:36
  84.3 0.0 copy-start
  84.4 2.0 copy-done
  86.4 3.7 %fusion.11 = f32[256,512]{1,0:T(8,128)S(1)} fusion(f32[2048,512]{1,0:T(8,128)S(1)} %bitcast.7, f32[512,2048]{1,0:T(8,128)S(1)} %constant_dynamic-update-slice_fusion, s32[]{:T(128)S(6)} %select_n.14), kind=kOutput, calls=%fused_computation.25 | convolution fusion | flops 3221225472 | bytes 6815748 | tf_op jit(solution)/shard_map/dot_general | solution.py:40
  90.1 0.9 pad_maximum_fusion.9
  91.0 0.0 reduce-scatter.3.cloned.1.call-update
  91.0 0.0 reduce-scatter.5.cloned.1.call-start
  91.1 26.5 %all_gather.6 = f32[256,512]{1,0:T(8,128)S(1)} all-gather(f32[32,512]{1,0:T(8,128)S(1)} %copy-done.4), channel_id=1, replica_groups=mesh['pix'=8,'tm'=4] {'pix'}, dimensions={0}, use_global_device_ids=true | all-gather | bytes 589824 | tf_op jit(solution)/shard_map/all_gather | solution.py:68
  117.6 25.6 %reduce-scatter.3.cloned.1.call-done = f32[32,768]{1,0:T(8,128)} async-done(((f32[256,768]{1,0:T(8,128)}), f32[32,768]{1,0:T(8,128)}) %reduce-scatter.3.cloned.1.call-update) | async-done | bytes 98320 | tf_op jit(solution)/shard_map/reduce_scatter | solution.py:70
  143.2 1.3 convolution_divide_fusion.1
  144.4 0.0 copy-start.5
  144.4 10.0 %all_gather.7 = f32[256,512]{1,0:T(8,128)S(1)} all-gather(f32[32,512]{1,0:T(8,128)S(1)} %convolution_divide_fusion.1), channel_id=1, replica_groups=mesh['pix'=8,'tm'=4] {'pix'}, dimensions={0}, use_global_device_ids=true | all-gather | bytes 589824 | tf_op jit(solution)/shard_map/all_gather | solution.py:79
  154.5 0.6 fusion.23
  155.1 5.5 %fusion.22 = f32[256,2048]{1,0:T(8,128)S(1)} fusion(f32[256,512]{1,0:T(8,128)S(1)} %all_gather.7, f32[2048,512]{1,0:T(8,128)} %bitcast.8), kind=kOutput, calls=%fused_computation.48 | convolution fusion | flops 3221225472 | bytes 6815744 | tf_op jit(solution)/shard_map/dot_general | solution.py:44
  160.6 1.6 pad_maximum_fusion.8
  162.3 0.0 reduce-scatter.5.cloned.1.call-update
  162.3 47.8 %reduce-scatter.5.cloned.1.call-done = f32[64,2304]{1,0:T(8,128)} async-done(((f32[256,2304]{1,0:T(8,128)}), f32[64,2304]{1,0:T(8,128)}) %reduce-scatter.5.cloned.1.call-update) | async-done | bytes 589840 | tf_op jit(solution)/shard_map/reduce_scatter | solution.py:81
  210.1 3.9 %convolution_divide_fusion = f32[64,2048]{1,0:T(8,128)} fusion(f32[512,2048]{1,0:T(8,128)} %copy-done.2, s32[]{:T(128)S(6)} %select_n.14, f32[64,2048]{1,0:T(8,128)S(1)} %copy-done.3, f32[64,2304]{1,0:T(8,128)} %reduce-scatter.5.cloned.1.call-done), kind=kOutput, calls=%fused_computation.21 | convolution fusion | flops 402915328 | bytes 3735556 | tf_op jit(solution)/shard_map/dot_general | solution.py:40
  (18 shorter events, 0.3 us)
Async XLA Ops:
  7.2 136.0 %reduce-scatter.3.cloned.1.call-start = ((), (), s32[]{:S(2)}) async-start(), calls=%async_computation.2 | async-start | bytes 884736 | tf_op jit(solution)/shard_map/reduce_scatter | solution.py:70
  8.5 7.5 %collective-permute-start.1 = (f32[1,256,512]{2,1,0:T(8,128)S(1)}, f32[1,256,512]{2,1,0:T(8,128)S(1)}, u32[]{:S(2)}, u32[]{:S(2)}) collective-permute-start(f32[1,256,512]{2,1,0:T(8,128)S(1)} %get-tuple-element.10), channel_id=1, source_target_pairs={{4,0},{8,4},{12,8},{16,12},{20,16},{24,20},{28,24},{5,1},{9,5},{13... | collective-permute-start | bytes 1572872 | tf_op jit(solution)/shard_map/ppermute | solution.py:20
  9.8 6.2 %collective-permute-start = (f32[1,256,512]{2,1,0:T(8,128)S(1)}, f32[1,256,512]{2,1,0:T(8,128)S(1)}, u32[]{:S(2)}, u32[]{:S(2)}) collective-permute-start(f32[1,256,512]{2,1,0:T(8,128)S(1)} %get-tuple-element.9), channel_id=1, source_target_pairs={{0,4},{4,8},{8,12},{12,16},{16,20},{20,24},{24,28},{1,5},{5,9},{9,... | collective-permute-start | bytes 1572872 | tf_op jit(solution)/shard_map/ppermute | solution.py:18
  12.9 23.5 %collective-permute-start.8 = (f32[64,2048]{1,0:T(8,128)}, f32[64,2048]{1,0:T(8,128)S(1)}, u32[]{:S(2)}, u32[]{:S(2)}) collective-permute-start(f32[64,2048]{1,0:T(8,128)} %param.4), channel_id=1, source_target_pairs={{0,1},{1,2},{2,3},{3,0},{4,5},{5,6},{6,7},{7,4},{8,9},{9,10},{10,1... | collective-permute-start | bytes 1572872 | tf_op jit(solution)/shard_map/ppermute | solution.py:64
  25.9 12.1 %collective-permute-start.3 = (f32[1,256,512]{2,1,0:T(8,128)S(1)}, f32[1,256,512]{2,1,0:T(8,128)S(1)}, u32[]{:S(2)}, u32[]{:S(2)}) collective-permute-start(f32[1,256,512]{2,1,0:T(8,128)S(1)} %get-tuple-element.8), channel_id=1, source_target_pairs={{4,0},{8,4},{12,8},{16,12},{20,16},{24,20},{28,24},{5,1},{9,5},{13... | collective-permute-start | bytes 1572872 | tf_op jit(solution)/shard_map/ppermute | solution.py:20
  27.2 10.8 %collective-permute-start.2 = (f32[1,256,512]{2,1,0:T(8,128)S(1)}, f32[1,256,512]{2,1,0:T(8,128)S(1)}, u32[]{:S(2)}, u32[]{:S(2)}) collective-permute-start(f32[1,256,512]{2,1,0:T(8,128)S(1)} %get-tuple-element.7), channel_id=1, source_target_pairs={{0,4},{4,8},{8,12},{12,16},{16,20},{20,24},{24,28},{1,5},{5,9},{9,... | collective-permute-start | bytes 1572872 | tf_op jit(solution)/shard_map/ppermute | solution.py:18
  36.3 18.3 %collective-permute-start.9 = (f32[64,2048]{1,0:T(8,128)S(1)}, f32[64,2048]{1,0:T(8,128)S(1)}, u32[]{:S(2)}, u32[]{:S(2)}) collective-permute-start(f32[64,2048]{1,0:T(8,128)S(1)} %collective-permute-done.8), channel_id=1, source_target_pairs={{0,1},{1,2},{2,3},{3,0},{4,5},{5,6},{6,7},{7,4},{8,9},{9,10},{10,1... | collective-permute-start | bytes 1572872 | tf_op jit(solution)/shard_map/ppermute | solution.py:64
  42.5 2.0 copy-start.1
  44.6 11.7 %collective-permute-start.5 = (f32[1,256,512]{2,1,0:T(8,128)S(1)}, f32[1,256,512]{2,1,0:T(8,128)S(1)}, u32[]{:S(2)}, u32[]{:S(2)}) collective-permute-start(f32[1,256,512]{2,1,0:T(8,128)S(1)} %get-tuple-element.6), channel_id=1, source_target_pairs={{4,0},{8,4},{12,8},{16,12},{20,16},{24,20},{28,24},{5,1},{9,5},{13... | collective-permute-start | bytes 1572872 | tf_op jit(solution)/shard_map/ppermute | solution.py:20
  45.9 10.4 %collective-permute-start.4 = (f32[1,256,512]{2,1,0:T(8,128)S(1)}, f32[1,256,512]{2,1,0:T(8,128)S(1)}, u32[]{:S(2)}, u32[]{:S(2)}) collective-permute-start(f32[1,256,512]{2,1,0:T(8,128)S(1)} %get-tuple-element.5), channel_id=1, source_target_pairs={{0,4},{4,8},{8,12},{12,16},{16,20},{20,24},{24,28},{1,5},{5,9},{9,... | collective-permute-start | bytes 1572872 | tf_op jit(solution)/shard_map/ppermute | solution.py:18
  54.7 22.8 %collective-permute-start.10 = (f32[64,2048]{1,0:T(8,128)S(1)}, f32[64,2048]{1,0:T(8,128)S(1)}, u32[]{:S(2)}, u32[]{:S(2)}) collective-permute-start(f32[64,2048]{1,0:T(8,128)S(1)} %collective-permute-done.9), channel_id=1, source_target_pairs={{0,1},{1,2},{2,3},{3,0},{4,5},{5,6},{6,7},{7,4},{8,9},{9,10},{10,1... | collective-permute-start | bytes 1572872 | tf_op jit(solution)/shard_map/ppermute | solution.py:64
  66.3 11.3 %copy-start.3 = (f32[64,2048]{1,0:T(8,128)S(1)}, f32[64,2048]{1,0:T(8,128)}, u32[]{:S(2)}) copy-start(f32[64,2048]{1,0:T(8,128)} %param.4) | copy-start | bytes 1572868
  66.4 13.3 %collective-permute-start.7 = (f32[1,256,512]{2,1,0:T(8,128)S(1)}, f32[1,256,512]{2,1,0:T(8,128)S(1)}, u32[]{:S(2)}, u32[]{:S(2)}) collective-permute-start(f32[1,256,512]{2,1,0:T(8,128)S(1)} %get-tuple-element.4), channel_id=1, source_target_pairs={{4,0},{8,4},{12,8},{16,12},{20,16},{24,20},{28,24},{5,1},{9,5},{13... | collective-permute-start | bytes 1572872 | tf_op jit(solution)/shard_map/ppermute | solution.py:20
  67.8 11.9 %collective-permute-start.6 = (f32[1,256,512]{2,1,0:T(8,128)S(1)}, f32[1,256,512]{2,1,0:T(8,128)S(1)}, u32[]{:S(2)}, u32[]{:S(2)}) collective-permute-start(f32[1,256,512]{2,1,0:T(8,128)S(1)} %get-tuple-element.3), channel_id=1, source_target_pairs={{0,4},{4,8},{8,12},{12,16},{16,20},{20,24},{24,28},{1,5},{5,9},{9,... | collective-permute-start | bytes 1572872 | tf_op jit(solution)/shard_map/ppermute | solution.py:18
  77.8 6.5 %copy-start.2 = (f32[512,2048]{1,0:T(8,128)}, f32[512,2048]{1,0:T(8,128)S(1)}, u32[]{:S(2)}) copy-start(f32[512,2048]{1,0:T(8,128)S(1)} %constant_dynamic-update-slice_fusion) | copy-start | bytes 12582916
  84.3 2.0 copy-start
  86.4 4.7 %copy-start.4 = (f32[32,512]{1,0:T(8,128)S(1)}, f32[32,512]{1,0:T(8,128)}, u32[]{:S(2)}) copy-start(f32[32,512]{1,0:T(8,128)} %param.5) | copy-start | bytes 196612
  91.0 119.1 %reduce-scatter.5.cloned.1.call-start = ((), (), s32[]{:S(2)}) async-start(), calls=%async_computation.3 | async-start | bytes 2949120 | tf_op jit(solution)/shard_map/reduce_scatter | solution.py:81
  144.4 16.2 %copy-start.5 = (f32[32,512]{1,0:T(8,128)}, f32[32,512]{1,0:T(8,128)S(1)}, u32[]{:S(2)}) copy-start(f32[32,512]{1,0:T(8,128)S(1)} %convolution_divide_fusion.1) | copy-start | bytes 196612
Sparse Core Ops, SparseCore 0:
  91.1 51.9 reduce-scatter.2
  162.4 47.6 reduce-scatter.4
